TPU v7x, 128 devices: a whole 4x4x4 slice. The times are simulated.
128 devices in a mesh: lat: 8 (over x, core), lon: 16 (over z, y).
Axes of the slice: x: 4, y: 4, z: 4, core: 2. Of those that a mesh axis runs over, the one named last changes fastest.
Arguments:
- prognostic_samples: float32 [40, 25, 64, 2048], P(None, None, 'lat', 'lon'), may hold values from -6 to 6
- wind: float32 [2, 64, 2048], P(None, 'lat', 'lon'), may hold values from -0.4 to 0.4
- obs_lat: int32 [2, 512], replicated, may hold values from 0 to 63
- obs_lon: int32 [2, 512], replicated, may hold values from 0 to 2047
- obs_var: int32 [2, 512], replicated, may hold values from 0 to 24
- obs_value: float32 [2, 512], replicated, may hold values from -6 to 6
- obs_error: float32 [2, 512], replicated, may hold values from 0.5 to 4
Outputs:
- analysis: float32 [40, 25, 64, 2048], P(None, None, 'lat', 'lon')
All inputs are finite; a program needn't handle non-finite values.
Results may differ from a plain program's by a relative error of at most 0.0001.
Values sent between devices are 32-bit elements; how exact they have to be, the bound alone decides.
A program may use at most 128 MiB of HBM per device.

v0:
```python
import jax
import jax.numpy as jnp
from jax import lax
from jax.sharding import PartitionSpec as P

STEPS = 2
BLOCK = 128
HIGHEST = lax.Precision.HIGHEST
DIFFUSE = 0.1


def with_halo(block, sides, width):
    for axis, dim in sides:
        count = lax.axis_size(axis)
        forward = [(i, i + 1) for i in range(count - 1)]
        forward.append((count - 1, 0))
        backward = [(target, source) for source, target in forward]
        low = lax.ppermute(
            lax.slice_in_dim(block, block.shape[dim] - width, None, axis=dim), axis, forward
        )
        high = lax.ppermute(lax.slice_in_dim(block, 0, width, axis=dim), axis, backward)
        block = jnp.concatenate([low, block, high], axis=dim)
    return block


def taper(scaled):
    inner_part = (
        ((-0.25 * scaled + 0.5) * scaled + 0.625) * scaled - 5.0 / 3.0
    ) * scaled * scaled + 1.0
    scaled_safe = jnp.maximum(scaled, 1.0)
    outer_part = (
        ((((scaled / 12.0 - 0.5) * scaled + 0.625) * scaled + 5.0 / 3.0) * scaled - 5.0) * scaled
        + 4.0
        - 2.0 / (3.0 * scaled_safe)
    )
    return jnp.where(scaled <= 1.0, inner_part, jnp.where(scaled < 2.0, outer_part, 0.0))


def taper_to(lat_a, lon_a, lat_b, lon_b, cycle_length, reach):
    meridional_spacing = (lat_a - lat_b).astype(jnp.float32)
    lon_gap = jnp.abs(lon_a - lon_b)
    lon_gap = jnp.minimum(lon_gap, cycle_length - lon_gap).astype(jnp.float32)
    return taper(jnp.sqrt(meridional_spacing * meridional_spacing + lon_gap * lon_gap) / reach)


def advance(padded, east_wind, north_wind):
    centre = padded[..., 1:-1, 1:-1]
    above_v = padded[..., 2:, 1:-1]
    below_v = padded[..., :-2, 1:-1]
    right_v = padded[..., 1:-1, 2:]
    left_v = padded[..., 1:-1, :-2]
    return (
        centre
        - 0.5 * east_wind * (right_v - left_v)
        - 0.5 * north_wind * (above_v - below_v)
        + DIFFUSE * (right_v + left_v + above_v + below_v - 4.0 * centre)
    )


def zero_outside_block(padded, margin):
    overall_line_count = padded.shape[-2]
    band_rows = overall_line_count - 2 * margin
    global_row = (
        lax.axis_index("lat") * band_rows - margin + lax.iota(jnp.int32, overall_line_count)
    )
    inside = (global_row >= 0) & (global_row < band_rows * lax.axis_size("lat"))
    return jnp.where(inside[:, None], padded, 0.0)


def gains(prior, values, errors):
    members = prior.shape[0]
    average = jnp.mean(prior, axis=0)
    anomaly = prior - average
    ensemble_spread = jnp.sum(anomaly * anomaly, axis=0) / (members - 1)
    total = ensemble_spread + errors
    weights = anomaly / ((members - 1) * total)
    shifts = values - average - anomaly / (1.0 + jnp.sqrt(errors / total))
    return (weights, shifts)


def read_priors(sample_realizations, sel_lat, sel_lon, sel_var, band_rows, band_cols):
    members, variables, cells = sample_realizations.shape
    local_lat = sel_lat - lax.axis_index("lat") * band_rows
    local_lon = sel_lon - lax.axis_index("lon") * band_cols
    owned = (local_lat >= 0) & (local_lat < band_rows) & (local_lon >= 0) & (local_lon < band_cols)
    position = (
        sel_var * cells
        + jnp.clip(local_lat, 0, band_rows - 1) * band_cols
        + jnp.clip(local_lon, 0, band_cols - 1)
    )
    picked = jnp.take(sample_realizations.reshape(members, variables * cells), position, axis=1)
    return jnp.where(owned[None, :], picked, 0.0)


def apply_block(sample_realizations, weights, shifts, damping_factors):
    projected = jnp.einsum("mvc,mk->vck", sample_realizations, weights, precision=HIGHEST)
    return sample_realizations + jnp.einsum(
        "vck,mk->mvc", projected * damping_factors, shifts, precision=HIGHEST
    )


def body(prognostic_samples, wind, obs_lat, obs_lon, obs_var, obs_value, obs_error):
    members, variables, band_rows, band_cols = prognostic_samples.shape
    state_now = prognostic_samples
    for section in range(STEPS):
        padded = with_halo(state_now, (("lat", 2), ("lon", 3)), 1)
        state_now = advance(zero_outside_block(padded, 1), wind[0], wind[1])
    sample_realizations = state_now.reshape(members, variables, band_rows * band_cols)
    cycle_length = band_cols * lax.axis_size("lon")
    reach = float(band_rows * lax.axis_size("lat") // 2)
    cell_ids = lax.iota(jnp.int32, band_rows * band_cols)
    cell_lat = (lax.axis_index("lat") * band_rows + cell_ids // band_cols)[:, None]
    cell_lon = (lax.axis_index("lon") * band_cols + cell_ids % band_cols)[:, None]
    block_count = obs_lat.shape[1] // BLOCK
    for batch_no in range(obs_lat.shape[0]):
        sel_lat = obs_lat[batch_no]
        sel_lon = obs_lon[batch_no]
        sel_var = obs_var[batch_no]
        values = obs_value[batch_no]
        errors = obs_error[batch_no]

        def block_slice(array, first_obs):
            return lax.dynamic_slice_in_dim(array, first_obs, BLOCK)

        def single_block(block_no, members_now):
            first_obs = block_no * BLOCK
            blk_lat = block_slice(sel_lat, first_obs)
            block_longitude = block_slice(sel_lon, first_obs)
            own_part = read_priors(
                members_now,
                blk_lat,
                block_longitude,
                block_slice(sel_var, first_obs),
                band_rows,
                band_cols,
            )
            prior = lax.psum(own_part, ("lat", "lon"))
            weights, shifts = gains(
                prior, block_slice(values, first_obs), block_slice(errors, first_obs)
            )
            damping_factors = taper_to(
                cell_lat, cell_lon, blk_lat[None, :], block_longitude[None, :], cycle_length, reach
            )
            return apply_block(members_now, weights, shifts, damping_factors)

        sample_realizations = lax.fori_loop(0, block_count, single_block, sample_realizations)
    return sample_realizations.reshape(members, variables, band_rows, band_cols)


def solution(mesh):
    in_specs = (P(None, None, "lat", "lon"), P(None, "lat", "lon"), P(), P(), P(), P(), P())
    out_specs = P(None, None, "lat", "lon")
    return jax.shard_map(body, mesh=mesh, in_specs=in_specs, out_specs=out_specs, check_vma=False)
```

profile of v0, /device:TPU:1, one launch (start us, length us, event | category | flops | bytes accessed | tf_op | source)
XLA Modules:
  0.0 1001.6 jit_solution(13554984503513488470)
XLA Ops:
  7.6 9.6 copy.111
  21.9 8.5 pad_maximum_fusion
  30.4 7.0 copy-done
  44.0 15.4 %copy.114 = f32[40,25,10,128]{3,0,2,1:T(8,128)} copy(f32[40,25,10,128]{0,1,3,2:T(8,128)} %copy-done) | data formatting | bytes 10240000 | tf_op jit(solution)/shard_map/concatenate | solution.py:22
  66.1 13.4 %maximum_select_fusion = f32[40,25,10,130]{3,0,2,1:T(8,128)} fusion(f32[40,25,10,1]{3,0,2,1:T(8,128)} %copy.115, f32[40,25,10,128]{3,0,2,1:T(8,128)} %copy.114, f32[40,25,10,1]{3,0,2,1:T(8,128)} %copy.113, pred[10]{0:T(512)(128)(4,1)S(1)} %compare_and_fusion.4), kind=kLoop, calls=%fused_computation.101 | loop fusion | flops 3900000 | bytes 10400010 | tf_op jit(solution)/shard_map/jit(_where)/select_n | solution.py:67
  79.4 14.2 %multiply_add_fusion.2 = f32[40,25,8,128]{3,0,2,1:T(8,128)S(1)} fusion(f32[40,25,10,130]{3,0,2,1:T(8,128)} %maximum_select_fusion, f32[8,128]{1,0:T(8,128)S(1)} %get-tuple-element.578, f32[8,128]{1,0:T(8,128)S(1)} %get-tuple-element.577), kind=kLoop, calls=%fused_computation.106 | loop fusion | flops 13312000 | bytes 24584192 | tf_op jit(solution)/shard_map/add | solution.py:53
  96.0 5.8 collective-permute-done.4
  105.0 5.5 fusion.59
  118.7 17.7 %collective-permute-start.7 = (f32[40,25,10,1]{0,1,3,2:T(8,128)S(1)}, f32[40,25,10,1]{0,1,3,2:T(8,128)S(1)}, u32[]{:S(2)}, u32[]{:S(2)}) collective-permute-start(f32[40,25,10,1]{0,1,3,2:T(8,128)S(1)} %copy.127), channel_id=1, source_target_pairs={{1,0},{2,1},{3,2},{4,3},{5,4},{6,5},{7,6},{8,7},{9,8},{10,9},{11,1... | collective-permute-start | bytes 120008 | tf_op jit(solution)/shard_map/ppermute | solution.py:21
  143.1 9.6 maximum_select_fusion.1
  152.7 5.7 copy_bitcast_fusion
  158.4 420.0 %while.32 = (s32[]{:T(128)}, f32[40,25,1024]{2,0,1:T(8,128)}, f32[512]{0:T(512)S(1)}, s32[512]{0:T(512)S(1)}, s32[512]{0:T(512)S(1)}, /*index=5*/s32[512]{0:T(51...) while((s32[]{:T(128)}, f32[40,25,1024]{2,0,1:T(8,128)}, ...), condition=%wide.region_4.6_spmd.clone, body=%wide.region_0.5_spmd.clone.sunk | while | flops 3155089920 | bytes 48024392 | solution.py:146
  158.6 9.1 copy.135
  173.2 67.1 %psum.32 = f32[40,128]{1,0:T(8,128)S(1)} all-reduce(f32[40,128]{1,0:T(8,128)S(1)} %bitcast_select_fusion.4), channel_id=1, replica_groups=mesh['lat'=8,'lon'=16] {'lat','lon'}, use_global_device_ids=true, to_apply=%region_1.2 | all-reduce | flops 5120 | bytes 40960 | tf_op jit(solution)/shard_map/while/body/eval_jaxpr/psum | solution.py:137
  240.5 14.2 %fusion.86 = f32[128,25,1024]{2,0,1:T(8,128)S(1)} fusion(f32[40,25,1024]{2,0,1:T(8,128)} %get-tuple-element.762, f32[40,128]{1,0:T(8,128)S(1)} %psum.32, f32[128]{0:T(128)S(1)} %get-tuple-element.718, f32[128]{0:T(128)S(1)} %get-tuple-element.717), kind=kOutput, calls=%fused_computation.22.clone.1 | convolution fusion | flops 1572874240 | bytes 17224704 | tf_op jit(solution)/shard_map/while/body/eval_jaxpr/mvc,mk->vck/dot_general | solution.py:96
  255.7 10.6 %fusion.89 = f32[40,25,1024]{2,0,1:T(8,128)} fusion(f32[40,25,1024]{2,0,1:T(8,128)} %get-tuple-element.762, f32[128,25,1024]{2,0,1:T(8,128)S(1)} %fusion.86, f32[1024,128]{0,1:T(8,128)S(1)} %fusion.88, f32[40,128]{1,0:T(8,128)S(1)} %psum.32, f32[128]{0:T(128)S(1)} %get-tuple-element.721, f32[128]{0:T(128)S(1)} %get-tuple-element.717, ...), kind=kOutput, calls=%fused_computation.9.clone.1 | convolution fusion | flops 1577180160 | bytes 21845504 | tf_op jit(solution)/shard_map/while/body/eval_jaxpr/vck,mk->mvc/dot_general | solution.py:97
  266.5 9.1 copy.135
  275.6 5.4 gather_fusion
  281.1 63.1 %psum.32 = f32[40,128]{1,0:T(8,128)S(1)} all-reduce(f32[40,128]{1,0:T(8,128)S(1)} %bitcast_select_fusion.4), channel_id=1, replica_groups=mesh['lat'=8,'lon'=16] {'lat','lon'}, use_global_device_ids=true, to_apply=%region_1.2 | all-reduce | flops 5120 | bytes 40960 | tf_op jit(solution)/shard_map/while/body/eval_jaxpr/psum | solution.py:137
  344.4 14.2 %fusion.86 = f32[128,25,1024]{2,0,1:T(8,128)S(1)} fusion(f32[40,25,1024]{2,0,1:T(8,128)} %get-tuple-element.762, f32[40,128]{1,0:T(8,128)S(1)} %psum.32, f32[128]{0:T(128)S(1)} %get-tuple-element.718, f32[128]{0:T(128)S(1)} %get-tuple-element.717), kind=kOutput, calls=%fused_computation.22.clone.1 | convolution fusion | flops 1572874240 | bytes 17224704 | tf_op jit(solution)/shard_map/while/body/eval_jaxpr/mvc,mk->vck/dot_general | solution.py:96
  359.5 10.6 %fusion.89 = f32[40,25,1024]{2,0,1:T(8,128)} fusion(f32[40,25,1024]{2,0,1:T(8,128)} %get-tuple-element.762, f32[128,25,1024]{2,0,1:T(8,128)S(1)} %fusion.86, f32[1024,128]{0,1:T(8,128)S(1)} %fusion.88, f32[40,128]{1,0:T(8,128)S(1)} %psum.32, f32[128]{0:T(128)S(1)} %get-tuple-element.721, f32[128]{0:T(128)S(1)} %get-tuple-element.717, ...), kind=kOutput, calls=%fused_computation.9.clone.1 | convolution fusion | flops 1577180160 | bytes 21845504 | tf_op jit(solution)/shard_map/while/body/eval_jaxpr/vck,mk->mvc/dot_general | solution.py:97
  370.3 9.1 copy.135
  379.4 5.4 gather_fusion
  384.9 64.0 %psum.32 = f32[40,128]{1,0:T(8,128)S(1)} all-reduce(f32[40,128]{1,0:T(8,128)S(1)} %bitcast_select_fusion.4), channel_id=1, replica_groups=mesh['lat'=8,'lon'=16] {'lat','lon'}, use_global_device_ids=true, to_apply=%region_1.2 | all-reduce | flops 5120 | bytes 40960 | tf_op jit(solution)/shard_map/while/body/eval_jaxpr/psum | solution.py:137
  449.1 14.2 %fusion.86 = f32[128,25,1024]{2,0,1:T(8,128)S(1)} fusion(f32[40,25,1024]{2,0,1:T(8,128)} %get-tuple-element.762, f32[40,128]{1,0:T(8,128)S(1)} %psum.32, f32[128]{0:T(128)S(1)} %get-tuple-element.718, f32[128]{0:T(128)S(1)} %get-tuple-element.717), kind=kOutput, calls=%fused_computation.22.clone.1 | convolution fusion | flops 1572874240 | bytes 17224704 | tf_op jit(solution)/shard_map/while/body/eval_jaxpr/mvc,mk->vck/dot_general | solution.py:96
  464.3 10.6 %fusion.89 = f32[40,25,1024]{2,0,1:T(8,128)} fusion(f32[40,25,1024]{2,0,1:T(8,128)} %get-tuple-element.762, f32[128,25,1024]{2,0,1:T(8,128)S(1)} %fusion.86, f32[1024,128]{0,1:T(8,128)S(1)} %fusion.88, f32[40,128]{1,0:T(8,128)S(1)} %psum.32, f32[128]{0:T(128)S(1)} %get-tuple-element.721, f32[128]{0:T(128)S(1)} %get-tuple-element.717, ...), kind=kOutput, calls=%fused_computation.9.clone.1 | convolution fusion | flops 1577180160 | bytes 21845504 | tf_op jit(solution)/shard_map/while/body/eval_jaxpr/vck,mk->mvc/dot_general | solution.py:97
  475.0 9.1 copy.135
  489.6 62.8 %psum.32 = f32[40,128]{1,0:T(8,128)S(1)} all-reduce(f32[40,128]{1,0:T(8,128)S(1)} %bitcast_select_fusion.4), channel_id=1, replica_groups=mesh['lat'=8,'lon'=16] {'lat','lon'}, use_global_device_ids=true, to_apply=%region_1.2 | all-reduce | flops 5120 | bytes 40960 | tf_op jit(solution)/shard_map/while/body/eval_jaxpr/psum | solution.py:137
  552.7 14.2 %fusion.86 = f32[128,25,1024]{2,0,1:T(8,128)S(1)} fusion(f32[40,25,1024]{2,0,1:T(8,128)} %get-tuple-element.762, f32[40,128]{1,0:T(8,128)S(1)} %psum.32, f32[128]{0:T(128)S(1)} %get-tuple-element.718, f32[128]{0:T(128)S(1)} %get-tuple-element.717), kind=kOutput, calls=%fused_computation.22.clone.1 | convolution fusion | flops 1572874240 | bytes 17224704 | tf_op jit(solution)/shard_map/while/body/eval_jaxpr/mvc,mk->vck/dot_general | solution.py:96
  567.8 10.6 %fusion.89 = f32[40,25,1024]{2,0,1:T(8,128)} fusion(f32[40,25,1024]{2,0,1:T(8,128)} %get-tuple-element.762, f32[128,25,1024]{2,0,1:T(8,128)S(1)} %fusion.86, f32[1024,128]{0,1:T(8,128)S(1)} %fusion.88, f32[40,128]{1,0:T(8,128)S(1)} %psum.32, f32[128]{0:T(128)S(1)} %get-tuple-element.721, f32[128]{0:T(128)S(1)} %get-tuple-element.717, ...), kind=kOutput, calls=%fused_computation.9.clone.1 | convolution fusion | flops 1577180160 | bytes 21845504 | tf_op jit(solution)/shard_map/while/body/eval_jaxpr/vck,mk->mvc/dot_general | solution.py:97
  578.5 417.4 %while.33 = (s32[]{:T(128)}, f32[40,25,1024]{2,0,1:T(8,128)}, f32[512]{0:T(512)S(1)}, s32[512]{0:T(512)S(1)}, s32[512]{0:T(512)S(1)}, /*index=5*/s32[512]{0:T(51...) while((s32[]{:T(128)}, f32[40,25,1024]{2,0,1:T(8,128)}, ...), condition=%wide.region_9.11_spmd.clone, body=%wide.region_5.10_spmd.clone.sunk | while | flops 3155089920 | bytes 48024392 | solution.py:146
  578.8 9.1 copy.137
  593.4 64.3 %psum.33 = f32[40,128]{1,0:T(8,128)S(1)} all-reduce(f32[40,128]{1,0:T(8,128)S(1)} %bitcast_select_fusion.5), channel_id=1, replica_groups=mesh['lat'=8,'lon'=16] {'lat','lon'}, use_global_device_ids=true, to_apply=%region_6.7 | all-reduce | flops 5120 | bytes 40960 | tf_op jit(solution)/shard_map/while/body/eval_jaxpr/psum | solution.py:137
  657.9 14.2 %fusion.93 = f32[128,25,1024]{2,0,1:T(8,128)S(1)} fusion(f32[40,25,1024]{2,0,1:T(8,128)} %get-tuple-element.816, f32[40,128]{1,0:T(8,128)S(1)} %psum.33, f32[128]{0:T(128)S(1)} %get-tuple-element.738, f32[128]{0:T(128)S(1)} %get-tuple-element.737), kind=kOutput, calls=%fused_computation.69.clone.1 | convolution fusion | flops 1572874240 | bytes 17224704 | tf_op jit(solution)/shard_map/while/body/eval_jaxpr/mvc,mk->vck/dot_general | solution.py:96
  673.1 10.6 %fusion.96 = f32[40,25,1024]{2,0,1:T(8,128)} fusion(f32[40,25,1024]{2,0,1:T(8,128)} %get-tuple-element.816, f32[128,25,1024]{2,0,1:T(8,128)S(1)} %fusion.93, f32[1024,128]{0,1:T(8,128)S(1)} %fusion.95, f32[40,128]{1,0:T(8,128)S(1)} %psum.33, f32[128]{0:T(128)S(1)} %get-tuple-element.741, f32[128]{0:T(128)S(1)} %get-tuple-element.737, ...), kind=kOutput, calls=%fused_computation.56.clone.1 | convolution fusion | flops 1577180160 | bytes 21845504 | tf_op jit(solution)/shard_map/while/body/eval_jaxpr/vck,mk->mvc/dot_general | solution.py:97
  683.9 9.1 copy.137
  698.5 62.8 %psum.33 = f32[40,128]{1,0:T(8,128)S(1)} all-reduce(f32[40,128]{1,0:T(8,128)S(1)} %bitcast_select_fusion.5), channel_id=1, replica_groups=mesh['lat'=8,'lon'=16] {'lat','lon'}, use_global_device_ids=true, to_apply=%region_6.7 | all-reduce | flops 5120 | bytes 40960 | tf_op jit(solution)/shard_map/while/body/eval_jaxpr/psum | solution.py:137
  761.5 14.2 %fusion.93 = f32[128,25,1024]{2,0,1:T(8,128)S(1)} fusion(f32[40,25,1024]{2,0,1:T(8,128)} %get-tuple-element.816, f32[40,128]{1,0:T(8,128)S(1)} %psum.33, f32[128]{0:T(128)S(1)} %get-tuple-element.738, f32[128]{0:T(128)S(1)} %get-tuple-element.737), kind=kOutput, calls=%fused_computation.69.clone.1 | convolution fusion | flops 1572874240 | bytes 17224704 | tf_op jit(solution)/shard_map/while/body/eval_jaxpr/mvc,mk->vck/dot_general | solution.py:96
  776.7 10.6 %fusion.96 = f32[40,25,1024]{2,0,1:T(8,128)} fusion(f32[40,25,1024]{2,0,1:T(8,128)} %get-tuple-element.816, f32[128,25,1024]{2,0,1:T(8,128)S(1)} %fusion.93, f32[1024,128]{0,1:T(8,128)S(1)} %fusion.95, f32[40,128]{1,0:T(8,128)S(1)} %psum.33, f32[128]{0:T(128)S(1)} %get-tuple-element.741, f32[128]{0:T(128)S(1)} %get-tuple-element.737, ...), kind=kOutput, calls=%fused_computation.56.clone.1 | convolution fusion | flops 1577180160 | bytes 21845504 | tf_op jit(solution)/shard_map/while/body/eval_jaxpr/vck,mk->mvc/dot_general | solution.py:97
  787.4 9.1 copy.137
  802.0 64.3 %psum.33 = f32[40,128]{1,0:T(8,128)S(1)} all-reduce(f32[40,128]{1,0:T(8,128)S(1)} %bitcast_select_fusion.5), channel_id=1, replica_groups=mesh['lat'=8,'lon'=16] {'lat','lon'}, use_global_device_ids=true, to_apply=%region_6.7 | all-reduce | flops 5120 | bytes 40960 | tf_op jit(solution)/shard_map/while/body/eval_jaxpr/psum | solution.py:137
  866.5 14.2 %fusion.93 = f32[128,25,1024]{2,0,1:T(8,128)S(1)} fusion(f32[40,25,1024]{2,0,1:T(8,128)} %get-tuple-element.816, f32[40,128]{1,0:T(8,128)S(1)} %psum.33, f32[128]{0:T(128)S(1)} %get-tuple-element.738, f32[128]{0:T(128)S(1)} %get-tuple-element.737), kind=kOutput, calls=%fused_computation.69.clone.1 | convolution fusion | flops 1572874240 | bytes 17224704 | tf_op jit(solution)/shard_map/while/body/eval_jaxpr/mvc,mk->vck/dot_general | solution.py:96
  881.7 10.6 %fusion.96 = f32[40,25,1024]{2,0,1:T(8,128)} fusion(f32[40,25,1024]{2,0,1:T(8,128)} %get-tuple-element.816, f32[128,25,1024]{2,0,1:T(8,128)S(1)} %fusion.93, f32[1024,128]{0,1:T(8,128)S(1)} %fusion.95, f32[40,128]{1,0:T(8,128)S(1)} %psum.33, f32[128]{0:T(128)S(1)} %get-tuple-element.741, f32[128]{0:T(128)S(1)} %get-tuple-element.737, ...), kind=kOutput, calls=%fused_computation.56.clone.1 | convolution fusion | flops 1577180160 | bytes 21845504 | tf_op jit(solution)/shard_map/while/body/eval_jaxpr/vck,mk->mvc/dot_general | solution.py:97
  892.5 9.1 copy.137
  901.6 5.4 gather_fusion.1
  907.1 62.8 %psum.33 = f32[40,128]{1,0:T(8,128)S(1)} all-reduce(f32[40,128]{1,0:T(8,128)S(1)} %bitcast_select_fusion.5), channel_id=1, replica_groups=mesh['lat'=8,'lon'=16] {'lat','lon'}, use_global_device_ids=true, to_apply=%region_6.7 | all-reduce | flops 5120 | bytes 40960 | tf_op jit(solution)/shard_map/while/body/eval_jaxpr/psum | solution.py:137
  970.1 14.2 %fusion.93 = f32[128,25,1024]{2,0,1:T(8,128)S(1)} fusion(f32[40,25,1024]{2,0,1:T(8,128)} %get-tuple-element.816, f32[40,128]{1,0:T(8,128)S(1)} %psum.33, f32[128]{0:T(128)S(1)} %get-tuple-element.738, f32[128]{0:T(128)S(1)} %get-tuple-element.737), kind=kOutput, calls=%fused_computation.69.clone.1 | convolution fusion | flops 1572874240 | bytes 17224704 | tf_op jit(solution)/shard_map/while/body/eval_jaxpr/mvc,mk->vck/dot_general | solution.py:96
  985.3 10.6 %fusion.96 = f32[40,25,1024]{2,0,1:T(8,128)} fusion(f32[40,25,1024]{2,0,1:T(8,128)} %get-tuple-element.816, f32[128,25,1024]{2,0,1:T(8,128)S(1)} %fusion.93, f32[1024,128]{0,1:T(8,128)S(1)} %fusion.95, f32[40,128]{1,0:T(8,128)S(1)} %psum.33, f32[128]{0:T(128)S(1)} %get-tuple-element.741, f32[128]{0:T(128)S(1)} %get-tuple-element.737, ...), kind=kOutput, calls=%fused_computation.56.clone.1 | convolution fusion | flops 1577180160 | bytes 21845504 | tf_op jit(solution)/shard_map/while/body/eval_jaxpr/vck,mk->mvc/dot_general | solution.py:97
  (145 shorter events, 89.1 us)
Async XLA Ops:
  4.2 13.1 %collective-permute-start = (f32[40,25,1,128]{3,0,2,1:T(8,128)S(1)}, f32[40,25,1,128]{3,0,2,1:T(8,128)S(1)}, u32[]{:S(2)}, u32[]{:S(2)}) collective-permute-start(f32[40,25,1,128]{3,0,2,1:T(8,128)S(1)} %copy.124), channel_id=1, source_target_pairs={{0,16},{16,32},{32,48},{48,64},{64,80},{80,96},{96,112},{112,0},{1... | collective-permute-start | bytes 1536008 | tf_op jit(solution)/shard_map/ppermute | solution.py:18
  7.6 9.6 copy-start.3
  7.6 9.6 copy-start.2
  7.6 11.5 %collective-permute-start.1 = (f32[40,25,1,128]{3,0,2,1:T(8,128)}, f32[40,25,1,128]{3,0,2,1:T(8,128)S(1)}, u32[]{:S(2)}, u32[]{:S(2)}) collective-permute-start(f32[40,25,1,128]{3,0,2,1:T(8,128)} %copy.125), channel_id=1, source_target_pairs={{16,0},{32,16},{48,32},{64,48},{80,64},{96,80},{112,96},{0,112},{1... | collective-permute-start | bytes 1536008 | tf_op jit(solution)/shard_map/ppermute | solution.py:21
  30.4 7.0 copy-start
  37.4 22.0 %collective-permute-start.2 = (f32[40,25,10,1]{0,1,3,2:T(8,128)S(1)}, f32[40,25,10,1]{0,1,3,2:T(8,128)S(1)}, u32[]{:S(2)}, u32[]{:S(2)}) collective-permute-start(f32[40,25,10,1]{0,1,3,2:T(8,128)S(1)} %get-tuple-element.569), channel_id=1, source_target_pairs={{0,1},{1,2},{2,3},{3,4},{4,5},{5,6},{6,7},{7,8},{8,9},{9,10},{10,1... | collective-permute-start | bytes 120008 | tf_op jit(solution)/shard_map/ppermute | solution.py:18
  38.7 24.0 %collective-permute-start.3 = (f32[40,25,10,1]{0,1,3,2:T(8,128)S(1)}, f32[40,25,10,1]{0,1,3,2:T(8,128)S(1)}, u32[]{:S(2)}, u32[]{:S(2)}) collective-permute-start(f32[40,25,10,1]{0,1,3,2:T(8,128)S(1)} %get-tuple-element.570), channel_id=1, source_target_pairs={{1,0},{2,1},{3,2},{4,3},{5,4},{6,5},{7,6},{8,7},{9,8},{10,9},{11,1... | collective-permute-start | bytes 120008 | tf_op jit(solution)/shard_map/ppermute | solution.py:21
  79.4 16.5 %copy-start.4 = (s32[2,512]{1,0:T(2,128)S(1)}, s32[2,512]{1,0:T(2,128)}, u32[]{:S(2)}) copy-start(s32[2,512]{1,0:T(2,128)} %param.15) | copy-start | bytes 12292
  79.4 16.5 %copy-start.5 = (s32[2,512]{1,0:T(2,128)S(1)}, s32[2,512]{1,0:T(2,128)}, u32[]{:S(2)}) copy-start(s32[2,512]{1,0:T(2,128)} %param.16) | copy-start | bytes 12292
  79.4 16.5 %copy-start.6 = (s32[2,512]{1,0:T(2,128)S(1)}, s32[2,512]{1,0:T(2,128)}, u32[]{:S(2)}) copy-start(s32[2,512]{1,0:T(2,128)} %param.17) | copy-start | bytes 12292
  93.7 11.3 %copy-start.1 = (f32[40,25,8,128]{3,0,2,1:T(8,128)}, f32[40,25,8,128]{3,0,2,1:T(8,128)S(1)}, u32[]{:S(2)}) copy-start(f32[40,25,8,128]{3,0,2,1:T(8,128)S(1)} %multiply_add_fusion.2) | copy-start | bytes 12288004
  93.8 8.0 collective-permute-start.4
  95.8 8.8 collective-permute-start.5
  110.5 25.9 %copy-start.7 = (f32[2,512]{1,0:T(2,128)S(1)}, f32[2,512]{1,0:T(2,128)}, u32[]{:S(2)}) copy-start(f32[2,512]{1,0:T(2,128)} %param.19) | copy-start | bytes 12292
  114.6 21.8 %collective-permute-start.6 = (f32[40,25,10,1]{0,1,3,2:T(8,128)S(1)}, f32[40,25,10,1]{0,1,3,2:T(8,128)S(1)}, u32[]{:S(2)}, u32[]{:S(2)}) collective-permute-start(f32[40,25,10,1]{0,1,3,2:T(8,128)S(1)} %copy.126), channel_id=1, source_target_pairs={{0,1},{1,2},{2,3},{3,4},{4,5},{5,6},{6,7},{7,8},{8,9},{9,10},{10,1... | collective-permute-start | bytes 120008 | tf_op jit(solution)/shard_map/ppermute | solution.py:18
  118.7 21.0 %collective-permute-start.7 = (f32[40,25,10,1]{0,1,3,2:T(8,128)S(1)}, f32[40,25,10,1]{0,1,3,2:T(8,128)S(1)}, u32[]{:S(2)}, u32[]{:S(2)}) collective-permute-start(f32[40,25,10,1]{0,1,3,2:T(8,128)S(1)} %copy.127), channel_id=1, source_target_pairs={{1,0},{2,1},{3,2},{4,3},{5,4},{6,5},{7,6},{8,7},{9,8},{10,9},{11,1... | collective-permute-start | bytes 120008 | tf_op jit(solution)/shard_map/ppermute | solution.py:21
where the time goes:
time: 1010 us; the launch traced here: 1000 us
  blocking collectives  511 us (51%)
  matrix products  199 us (20%)
  local copies, waits for them, and re-layouts  190 us (19%)
  other arithmetic  62.4 us (6%)
  starting transfers between devices  29.1 us (3%)
    psum x8, blocking collectives, single_block(): prior = lax.psum(own_part, ('lat', 'lon'))  511 us
    dot_general x8, matrix products, apply_block(): jnp.einsum('mvc,mk->vck', sample_realizations, weights, precision=HIGHEST)  114 us
    dot_general x8, matrix products, apply_block(): jnp.einsum('vck,mk->mvc', projected * damping_factors, shifts, precision=...  84.9 us
    while x8, local copies, waits for them, and re-layouts  73 us
    gather x16, local copies, waits for them, and re-layouts, read_priors(): jnp.take(sample_realizations.reshape(members, variables * cells), positio...  43.4 us
    unnamed x22, local copies, waits for them, and re-layouts  28.7 us
    ppermute x4, starting transfers between devices, with_halo(): lax.ppermute(lax.slice_in_dim(block, 0, width, axis=dim), axis, backward)  23.1 us
    select_n x2, other arithmetic, zero_outside_block(): return jnp.where(inside[:, None], padded, 0.0)  23 us
  transfers between devices with their start and end apart: 8, of which 2 were waited for; matrix products, arithmetic and copies ran while one was open for 4% of the time, Pallas kernels for 0%

commit v1 on v0

--- a/solution.py
+++ b/solution.py
@@ -134,7 +134,7 @@
                 band_rows,
                 band_cols,
             )
-            prior = lax.psum(own_part, ("lat", "lon"))
+            prior = jnp.sum(lax.all_gather(own_part, ("lat", "lon")), axis=0)
             weights, shifts = gains(
                 prior, block_slice(values, first_obs), block_slice(errors, first_obs)
             )

time: 1010 us -> 1040 us (1.030)
  blocking collectives: 511 us -> 0 us
  waiting for transfers between devices: 8.6 us -> 510 us
  other arithmetic: 62.4 us -> 88 us
  local copies, waits for them, and re-layouts: 190 us -> 215 us
  between operations: 0.58 us -> 13.9 us
  starting transfers between devices: 29.1 us -> 16.7 us
  matrix products: 199 us -> 188 us
    psum x8 -> x0, blocking collectives: 511 us -> none  [single_block(): prior = lax.psum(own_part, ('lat', 'lon'))]
    all_gather x0 -> x8, waiting for transfers between devices: none -> 501 us  [single_block(): prior = jnp.sum(lax.all_gather(own_part, ('lat', 'lon')), axis=0)]
    while x8 -> x56, local copies, waits for them, and re-layouts: 73 us -> 92.2 us
    reduce_sum x0 -> x8, other arithmetic: none -> 16.8 us  [single_block(): prior = jnp.sum(lax.all_gather(own_part, ('lat', 'lon')), axis=0)]
    ppermute x4, starting transfers between devices: 23.1 us -> 10.6 us  [with_halo(): lax.ppermute(lax.slice_in_dim(block, 0, width, axis=dim), axis, backward)]
    dot_general x8, matrix products: 84.9 us -> 73.4 us  [apply_block(): jnp.einsum('vck,mk->mvc', projected * damping_factors, shifts, precision=...]
    gather x16 -> x8, local copies, waits for them, and re-layouts: 43.4 us -> 43 us  [read_priors(): jnp.take(sample_realizations.reshape(members, variables * cells), positio...]
  transfers between devices with their start and end apart: 8 -> 16, of which waited for: 2 -> 10; matrix products, arithmetic and copies ran while one was open for 4% -> 4% of each run, Pallas kernels for 0% -> 0%
where the time goes in v1:
time: 1040 us; the launch traced here: 1030 us
  waiting for transfers between devices  510 us (49%)
  local copies, waits for them, and re-layouts  215 us (21%)
  matrix products  188 us (18%)
  other arithmetic  88 us (8%)
  starting transfers between devices  16.7 us (2%)
  between operations  13.9 us (1%)
    all_gather x8, waiting for transfers between devices, single_block(): prior = jnp.sum(lax.all_gather(own_part, ('lat', 'lon')), axis=0)  501 us
    dot_general x8, matrix products, apply_block(): jnp.einsum('mvc,mk->vck', sample_realizations, weights, precision=HIGHEST)  115 us
    while x56, local copies, waits for them, and re-layouts  92.2 us
    dot_general x8, matrix products, apply_block(): jnp.einsum('vck,mk->mvc', projected * damping_factors, shifts, precision=...  73.4 us
    gather x8, local copies, waits for them, and re-layouts, read_priors(): jnp.take(sample_realizations.reshape(members, variables * cells), positio...  43 us
    unnamed x22, local copies, waits for them, and re-layouts  28.7 us
    select_n x2, other arithmetic, zero_outside_block(): return jnp.where(inside[:, None], padded, 0.0)  23 us
  transfers between devices with their start and end apart: 16, of which 10 were waited for; matrix products, arithmetic and copies ran while one was open for 4% of the time, Pallas kernels for 0%

profile of v1, /device:TPU:1, one launch (start us, length us, event | category | flops | bytes accessed | tf_op | source)
XLA Modules:
  0.0 1032.9 jit_solution(5691756345463620665)
XLA Ops:
  14.1 9.6 copy.81
  29.0 8.5 pad_maximum_fusion
  37.5 7.0 copy-done.6
  51.1 15.4 %copy.84 = f32[40,25,10,128]{3,0,2,1:T(8,128)} copy(f32[40,25,10,128]{0,1,3,2:T(8,128)} %copy-done.6) | data formatting | bytes 10240000 | tf_op jit(solution)/shard_map/concatenate | solution.py:22
  73.2 13.4 %maximum_select_fusion = f32[40,25,10,130]{3,0,2,1:T(8,128)} fusion(f32[40,25,10,1]{3,0,2,1:T(8,128)} %copy.85, f32[40,25,10,128]{3,0,2,1:T(8,128)} %copy.84, f32[40,25,10,1]{3,0,2,1:T(8,128)} %copy.83, pred[10]{0:T(512)(128)(4,1)S(1)} %compare_and_fusion.4), kind=kLoop, calls=%fused_computation.101 | loop fusion | flops 3900000 | bytes 10400010 | tf_op jit(solution)/shard_map/jit(_where)/select_n | solution.py:67
  86.6 14.3 %multiply_add_fusion.2 = f32[40,25,8,128]{3,0,2,1:T(8,128)S(1)} fusion(f32[40,25,10,130]{3,0,2,1:T(8,128)} %maximum_select_fusion, f32[8,128]{1,0:T(8,128)S(1)} %get-tuple-element.578, f32[8,128]{1,0:T(8,128)S(1)} %get-tuple-element.577), kind=kLoop, calls=%fused_computation.106 | loop fusion | flops 13312000 | bytes 24584192 | tf_op jit(solution)/shard_map/add | solution.py:53
  103.2 5.8 collective-permute-done.4
  112.2 5.5 fusion.59
  137.9 9.6 maximum_select_fusion.1
  147.6 5.7 copy_bitcast_fusion
  153.3 434.3 %while.32 = (s32[]{:T(128)}, f32[40,25,1024]{2,0,1:T(8,128)}, f32[512]{0:T(512)S(1)}, s32[512]{0:T(512)S(1)}, s32[512]{0:T(512)S(1)}, /*index=5*/s32[512]{0:T(51...) while((s32[]{:T(128)}, f32[40,25,1024]{2,0,1:T(8,128)}, ...), condition=%wide.region_4.6_spmd.clone, body=%wide.region_0.5_spmd.clone.sunk | while | flops 3156385280 | bytes 104405952 | solution.py:146
  153.7 9.1 copy.105
  169.9 66.3 %all-gather.11.cloned.1.call-done = f32[5120,128]{1,0:T(8,128)} async-done(((f32[40,128]{1,0:T(8,128)}), f32[5120,128]{1,0:T(8,128)}) %all-gather.11.cloned.1.call-update) | async-done | bytes 2621456 | tf_op jit(solution)/shard_map/while/body/eval_jaxpr/all_gather | solution.py:137
  239.7 14.4 %fusion.86 = f32[128,25,1024]{2,0,1:T(8,128)S(1)} fusion(f32[40,25,1024]{2,0,1:T(8,128)} %get-tuple-element.762, f32[40,128]{1,0:T(8,128)S(1)} %reduce_sum.111, f32[128]{0:T(128)S(1)} %get-tuple-element.718, f32[128]{0:T(128)S(1)} %get-tuple-element.717), kind=kOutput, calls=%fused_computation.23.clone.1 | convolution fusion | flops 1572874240 | bytes 17224704 | tf_op jit(solution)/shard_map/while/body/eval_jaxpr/mvc,mk->vck/dot_general | solution.py:96
  254.1 9.2 fusion.89
  265.4 9.1 copy.105
  274.5 5.4 gather_fusion
  281.6 62.1 %all-gather.11.cloned.1.call-done = f32[5120,128]{1,0:T(8,128)} async-done(((f32[40,128]{1,0:T(8,128)}), f32[5120,128]{1,0:T(8,128)}) %all-gather.11.cloned.1.call-update) | async-done | bytes 2621456 | tf_op jit(solution)/shard_map/while/body/eval_jaxpr/all_gather | solution.py:137
  347.1 14.4 %fusion.86 = f32[128,25,1024]{2,0,1:T(8,128)S(1)} fusion(f32[40,25,1024]{2,0,1:T(8,128)} %get-tuple-element.762, f32[40,128]{1,0:T(8,128)S(1)} %reduce_sum.111, f32[128]{0:T(128)S(1)} %get-tuple-element.718, f32[128]{0:T(128)S(1)} %get-tuple-element.717), kind=kOutput, calls=%fused_computation.23.clone.1 | convolution fusion | flops 1572874240 | bytes 17224704 | tf_op jit(solution)/shard_map/while/body/eval_jaxpr/mvc,mk->vck/dot_general | solution.py:96
  361.5 9.2 fusion.89
  372.8 9.1 copy.105
  389.1 62.1 %all-gather.11.cloned.1.call-done = f32[5120,128]{1,0:T(8,128)} async-done(((f32[40,128]{1,0:T(8,128)}), f32[5120,128]{1,0:T(8,128)}) %all-gather.11.cloned.1.call-update) | async-done | bytes 2621456 | tf_op jit(solution)/shard_map/while/body/eval_jaxpr/all_gather | solution.py:137
  454.6 14.4 %fusion.86 = f32[128,25,1024]{2,0,1:T(8,128)S(1)} fusion(f32[40,25,1024]{2,0,1:T(8,128)} %get-tuple-element.762, f32[40,128]{1,0:T(8,128)S(1)} %reduce_sum.111, f32[128]{0:T(128)S(1)} %get-tuple-element.718, f32[128]{0:T(128)S(1)} %get-tuple-element.717), kind=kOutput, calls=%fused_computation.23.clone.1 | convolution fusion | flops 1572874240 | bytes 17224704 | tf_op jit(solution)/shard_map/while/body/eval_jaxpr/mvc,mk->vck/dot_general | solution.py:96
  469.0 9.2 fusion.89
  480.3 9.1 copy.105
  489.4 5.4 gather_fusion
  496.5 62.1 %all-gather.11.cloned.1.call-done = f32[5120,128]{1,0:T(8,128)} async-done(((f32[40,128]{1,0:T(8,128)}), f32[5120,128]{1,0:T(8,128)}) %all-gather.11.cloned.1.call-update) | async-done | bytes 2621456 | tf_op jit(solution)/shard_map/while/body/eval_jaxpr/all_gather | solution.py:137
  562.0 14.4 %fusion.86 = f32[128,25,1024]{2,0,1:T(8,128)S(1)} fusion(f32[40,25,1024]{2,0,1:T(8,128)} %get-tuple-element.762, f32[40,128]{1,0:T(8,128)S(1)} %reduce_sum.111, f32[128]{0:T(128)S(1)} %get-tuple-element.718, f32[128]{0:T(128)S(1)} %get-tuple-element.717), kind=kOutput, calls=%fused_computation.23.clone.1 | convolution fusion | flops 1572874240 | bytes 17224704 | tf_op jit(solution)/shard_map/while/body/eval_jaxpr/mvc,mk->vck/dot_general | solution.py:96
  576.4 9.2 fusion.89
  587.6 432.7 %while.33 = (s32[]{:T(128)}, f32[40,25,1024]{2,0,1:T(8,128)}, f32[512]{0:T(512)}, s32[512]{0:T(512)S(1)}, s32[512]{0:T(512)S(1)}, /*index=5*/s32[512]{0:T(512)S(...) while((s32[]{:T(128)}, f32[40,25,1024]{2,0,1:T(8,128)}, ...), condition=%wide.region_9.11_spmd.clone, body=%wide.region_5.10_spmd.clone.sunk | while | flops 3156385280 | bytes 104405952 | solution.py:146
  588.0 9.1 copy.107
  604.3 62.1 %all-gather.13.cloned.1.call-done = f32[5120,128]{1,0:T(8,128)} async-done(((f32[40,128]{1,0:T(8,128)}), f32[5120,128]{1,0:T(8,128)}) %all-gather.13.cloned.1.call-update) | async-done | bytes 2621456 | tf_op jit(solution)/shard_map/while/body/eval_jaxpr/all_gather | solution.py:137
  670.4 14.4 %fusion.93 = f32[128,25,1024]{2,0,1:T(8,128)S(1)} fusion(f32[40,25,1024]{2,0,1:T(8,128)} %get-tuple-element.816, f32[40,128]{1,0:T(8,128)S(1)} %reduce_sum.114, f32[128]{0:T(128)S(1)} %get-tuple-element.738, f32[128]{0:T(128)S(1)} %get-tuple-element.737), kind=kOutput, calls=%fused_computation.70.clone.1 | convolution fusion | flops 1572874240 | bytes 17224704 | tf_op jit(solution)/shard_map/while/body/eval_jaxpr/mvc,mk->vck/dot_general | solution.py:96
  684.8 9.2 fusion.96
  696.1 9.1 copy.107
  705.3 5.4 gather_fusion.1
  712.4 62.1 %all-gather.13.cloned.1.call-done = f32[5120,128]{1,0:T(8,128)} async-done(((f32[40,128]{1,0:T(8,128)}), f32[5120,128]{1,0:T(8,128)}) %all-gather.13.cloned.1.call-update) | async-done | bytes 2621456 | tf_op jit(solution)/shard_map/while/body/eval_jaxpr/all_gather | solution.py:137
  778.5 14.4 %fusion.93 = f32[128,25,1024]{2,0,1:T(8,128)S(1)} fusion(f32[40,25,1024]{2,0,1:T(8,128)} %get-tuple-element.816, f32[40,128]{1,0:T(8,128)S(1)} %reduce_sum.114, f32[128]{0:T(128)S(1)} %get-tuple-element.738, f32[128]{0:T(128)S(1)} %get-tuple-element.737), kind=kOutput, calls=%fused_computation.70.clone.1 | convolution fusion | flops 1572874240 | bytes 17224704 | tf_op jit(solution)/shard_map/while/body/eval_jaxpr/mvc,mk->vck/dot_general | solution.py:96
  792.9 9.2 fusion.96
  804.3 9.1 copy.107
  820.5 62.1 %all-gather.13.cloned.1.call-done = f32[5120,128]{1,0:T(8,128)} async-done(((f32[40,128]{1,0:T(8,128)}), f32[5120,128]{1,0:T(8,128)}) %all-gather.13.cloned.1.call-update) | async-done | bytes 2621456 | tf_op jit(solution)/shard_map/while/body/eval_jaxpr/all_gather | solution.py:137
  886.6 14.4 %fusion.93 = f32[128,25,1024]{2,0,1:T(8,128)S(1)} fusion(f32[40,25,1024]{2,0,1:T(8,128)} %get-tuple-element.816, f32[40,128]{1,0:T(8,128)S(1)} %reduce_sum.114, f32[128]{0:T(128)S(1)} %get-tuple-element.738, f32[128]{0:T(128)S(1)} %get-tuple-element.737), kind=kOutput, calls=%fused_computation.70.clone.1 | convolution fusion | flops 1572874240 | bytes 17224704 | tf_op jit(solution)/shard_map/while/body/eval_jaxpr/mvc,mk->vck/dot_general | solution.py:96
  901.0 9.2 fusion.96
  912.4 9.1 copy.107
  921.5 5.4 gather_fusion.1
  928.6 62.1 %all-gather.13.cloned.1.call-done = f32[5120,128]{1,0:T(8,128)} async-done(((f32[40,128]{1,0:T(8,128)}), f32[5120,128]{1,0:T(8,128)}) %all-gather.13.cloned.1.call-update) | async-done | bytes 2621456 | tf_op jit(solution)/shard_map/while/body/eval_jaxpr/all_gather | solution.py:137
  994.8 14.4 %fusion.93 = f32[128,25,1024]{2,0,1:T(8,128)S(1)} fusion(f32[40,25,1024]{2,0,1:T(8,128)} %get-tuple-element.816, f32[40,128]{1,0:T(8,128)S(1)} %reduce_sum.114, f32[128]{0:T(128)S(1)} %get-tuple-element.738, f32[128]{0:T(128)S(1)} %get-tuple-element.737), kind=kOutput, calls=%fused_computation.70.clone.1 | convolution fusion | flops 1572874240 | bytes 17224704 | tf_op jit(solution)/shard_map/while/body/eval_jaxpr/mvc,mk->vck/dot_general | solution.py:96
  1009.2 9.2 fusion.96
  (217 shorter events, 139.5 us)
Async XLA Ops:
  10.7 13.6 %collective-permute-start = (f32[40,25,1,128]{3,0,2,1:T(8,128)S(1)}, f32[40,25,1,128]{3,0,2,1:T(8,128)S(1)}, u32[]{:S(2)}, u32[]{:S(2)}) collective-permute-start(f32[40,25,1,128]{3,0,2,1:T(8,128)S(1)} %copy.94), channel_id=1, source_target_pairs={{0,16},{16,32},{32,48},{48,64},{64,80},{80,96},{96,112},{112,0},{1... | collective-permute-start | bytes 1536008 | tf_op jit(solution)/shard_map/ppermute | solution.py:18
  14.1 9.6 copy-start.9
  14.1 10.2 copy-start.8
  14.1 12.1 %collective-permute-start.1 = (f32[40,25,1,128]{3,0,2,1:T(8,128)}, f32[40,25,1,128]{3,0,2,1:T(8,128)S(1)}, u32[]{:S(2)}, u32[]{:S(2)}) collective-permute-start(f32[40,25,1,128]{3,0,2,1:T(8,128)} %copy.95), channel_id=1, source_target_pairs={{16,0},{32,16},{48,32},{64,48},{80,64},{96,80},{112,96},{0,112},{1... | collective-permute-start | bytes 1536008 | tf_op jit(solution)/shard_map/ppermute | solution.py:21
  37.5 7.0 copy-start.6
  44.5 22.0 %collective-permute-start.2 = (f32[40,25,10,1]{0,1,3,2:T(8,128)S(1)}, f32[40,25,10,1]{0,1,3,2:T(8,128)S(1)}, u32[]{:S(2)}, u32[]{:S(2)}) collective-permute-start(f32[40,25,10,1]{0,1,3,2:T(8,128)S(1)} %get-tuple-element.569), channel_id=1, source_target_pairs={{0,1},{1,2},{2,3},{3,4},{4,5},{5,6},{6,7},{7,8},{8,9},{9,10},{10,1... | collective-permute-start | bytes 120008 | tf_op jit(solution)/shard_map/ppermute | solution.py:18
  45.9 24.1 %collective-permute-start.3 = (f32[40,25,10,1]{0,1,3,2:T(8,128)S(1)}, f32[40,25,10,1]{0,1,3,2:T(8,128)S(1)}, u32[]{:S(2)}, u32[]{:S(2)}) collective-permute-start(f32[40,25,10,1]{0,1,3,2:T(8,128)S(1)} %get-tuple-element.570), channel_id=1, source_target_pairs={{1,0},{2,1},{3,2},{4,3},{5,4},{6,5},{7,6},{8,7},{9,8},{10,9},{11,1... | collective-permute-start | bytes 120008 | tf_op jit(solution)/shard_map/ppermute | solution.py:21
  86.6 16.5 %copy-start.10 = (s32[2,512]{1,0:T(2,128)S(1)}, s32[2,512]{1,0:T(2,128)}, u32[]{:S(2)}) copy-start(s32[2,512]{1,0:T(2,128)} %param.15) | copy-start | bytes 12292
  86.6 16.6 %copy-start.11 = (s32[2,512]{1,0:T(2,128)S(1)}, s32[2,512]{1,0:T(2,128)}, u32[]{:S(2)}) copy-start(s32[2,512]{1,0:T(2,128)} %param.16) | copy-start | bytes 12292
  86.6 16.6 %copy-start.12 = (s32[2,512]{1,0:T(2,128)S(1)}, s32[2,512]{1,0:T(2,128)}, u32[]{:S(2)}) copy-start(s32[2,512]{1,0:T(2,128)} %param.17) | copy-start | bytes 12292
  100.9 11.3 %copy-start.7 = (f32[40,25,8,128]{3,0,2,1:T(8,128)}, f32[40,25,8,128]{3,0,2,1:T(8,128)S(1)}, u32[]{:S(2)}) copy-start(f32[40,25,8,128]{3,0,2,1:T(8,128)S(1)} %multiply_add_fusion.2) | copy-start | bytes 12288004
  101.0 8.0 collective-permute-start.4
  103.0 8.8 collective-permute-start.5
  117.8 13.4 %copy-start.13 = (f32[2,512]{1,0:T(2,128)S(1)}, f32[2,512]{1,0:T(2,128)}, u32[]{:S(2)}) copy-start(f32[2,512]{1,0:T(2,128)} %param.19) | copy-start | bytes 12292
  121.9 9.4 collective-permute-start.6
  126.0 8.6 collective-permute-start.7
  153.5 82.8 %all-gather.11.cloned.1.call-start = ((), (), s32[]{:S(2)}) async-start(), calls=%async_computation | async-start | bytes 2641920 | tf_op jit(solution)/shard_map/while/body/eval_jaxpr/all_gather | solution.py:137
  236.3 2.5 copy-start.4
  239.7 14.4 %copy-start = (f32[40,25,1024]{2,0,1:T(8,128)S(1)}, f32[40,25,1024]{2,0,1:T(8,128)}, u32[]{:S(2)}) copy-start(f32[40,25,1024]{2,0,1:T(8,128)} %get-tuple-element.762) | copy-start | bytes 12288004 | tf_op jit(solution)/shard_map/while
  263.2 2.0 copy-start.1
  265.2 78.5 %all-gather.11.cloned.1.call-start = ((), (), s32[]{:S(2)}) async-start(), calls=%async_computation | async-start | bytes 2641920 | tf_op jit(solution)/shard_map/while/body/eval_jaxpr/all_gather | solution.py:137
  343.7 2.5 copy-start.4
  347.1 14.4 %copy-start = (f32[40,25,1024]{2,0,1:T(8,128)S(1)}, f32[40,25,1024]{2,0,1:T(8,128)}, u32[]{:S(2)}) copy-start(f32[40,25,1024]{2,0,1:T(8,128)} %get-tuple-element.762) | copy-start | bytes 12288004 | tf_op jit(solution)/shard_map/while
  370.7 2.0 copy-start.1
  372.7 78.5 %all-gather.11.cloned.1.call-start = ((), (), s32[]{:S(2)}) async-start(), calls=%async_computation | async-start | bytes 2641920 | tf_op jit(solution)/shard_map/while/body/eval_jaxpr/all_gather | solution.py:137
  451.2 2.5 copy-start.4
  454.6 14.4 %copy-start = (f32[40,25,1024]{2,0,1:T(8,128)S(1)}, f32[40,25,1024]{2,0,1:T(8,128)}, u32[]{:S(2)}) copy-start(f32[40,25,1024]{2,0,1:T(8,128)} %get-tuple-element.762) | copy-start | bytes 12288004 | tf_op jit(solution)/shard_map/while
  478.1 2.0 copy-start.1
  480.1 78.5 %all-gather.11.cloned.1.call-start = ((), (), s32[]{:S(2)}) async-start(), calls=%async_computation | async-start | bytes 2641920 | tf_op jit(solution)/shard_map/while/body/eval_jaxpr/all_gather | solution.py:137
  558.6 2.5 copy-start.4
  562.0 14.4 %copy-start = (f32[40,25,1024]{2,0,1:T(8,128)S(1)}, f32[40,25,1024]{2,0,1:T(8,128)}, u32[]{:S(2)}) copy-start(f32[40,25,1024]{2,0,1:T(8,128)} %get-tuple-element.762) | copy-start | bytes 12288004 | tf_op jit(solution)/shard_map/while
  585.6 2.0 copy-start.1
  587.8 78.6 %all-gather.13.cloned.1.call-start = ((), (), s32[]{:S(2)}) async-start(), calls=%async_computation.1 | async-start | bytes 2641920 | tf_op jit(solution)/shard_map/while/body/eval_jaxpr/all_gather | solution.py:137
  666.3 2.5 copy-start.5
  670.4 14.4 %copy-start.2 = (f32[40,25,1024]{2,0,1:T(8,128)S(1)}, f32[40,25,1024]{2,0,1:T(8,128)}, u32[]{:S(2)}) copy-start(f32[40,25,1024]{2,0,1:T(8,128)} %get-tuple-element.816) | copy-start | bytes 12288004 | tf_op jit(solution)/shard_map/while
  694.0 2.0 copy-start.3
  696.0 78.5 %all-gather.13.cloned.1.call-start = ((), (), s32[]{:S(2)}) async-start(), calls=%async_computation.1 | async-start | bytes 2641920 | tf_op jit(solution)/shard_map/while/body/eval_jaxpr/all_gather | solution.py:137
  774.5 2.5 copy-start.5
  778.5 14.4 %copy-start.2 = (f32[40,25,1024]{2,0,1:T(8,128)S(1)}, f32[40,25,1024]{2,0,1:T(8,128)}, u32[]{:S(2)}) copy-start(f32[40,25,1024]{2,0,1:T(8,128)} %get-tuple-element.816) | copy-start | bytes 12288004 | tf_op jit(solution)/shard_map/while
  802.1 2.0 copy-start.3
  804.1 78.5 %all-gather.13.cloned.1.call-start = ((), (), s32[]{:S(2)}) async-start(), calls=%async_computation.1 | async-start | bytes 2641920 | tf_op jit(solution)/shard_map/while/body/eval_jaxpr/all_gather | solution.py:137
  882.6 2.5 copy-start.5
  886.6 14.4 %copy-start.2 = (f32[40,25,1024]{2,0,1:T(8,128)S(1)}, f32[40,25,1024]{2,0,1:T(8,128)}, u32[]{:S(2)}) copy-start(f32[40,25,1024]{2,0,1:T(8,128)} %get-tuple-element.816) | copy-start | bytes 12288004 | tf_op jit(solution)/shard_map/while
  910.2 2.0 copy-start.3
  912.2 78.5 %all-gather.13.cloned.1.call-start = ((), (), s32[]{:S(2)}) async-start(), calls=%async_computation.1 | async-start | bytes 2641920 | tf_op jit(solution)/shard_map/while/body/eval_jaxpr/all_gather | solution.py:137
  990.7 2.5 copy-start.5
  994.8 14.4 %copy-start.2 = (f32[40,25,1024]{2,0,1:T(8,128)S(1)}, f32[40,25,1024]{2,0,1:T(8,128)}, u32[]{:S(2)}) copy-start(f32[40,25,1024]{2,0,1:T(8,128)} %get-tuple-element.816) | copy-start | bytes 12288004 | tf_op jit(solution)/shard_map/while
  1018.3 2.0 copy-start.3
Sparse Core Ops, SparseCore 0:
  169.1 67.0 all-gather.10
  280.8 62.8 all-gather.10
  388.3 62.8 all-gather.10
  495.7 62.8 all-gather.10
  603.4 62.8 all-gather.12
  711.6 62.8 all-gather.12
  819.7 62.8 all-gather.12
  927.8 62.8 all-gather.12
